TPU v7x, 256 devices: a whole 4x4x8 slice. The times are simulated.
256 devices in a mesh: ma: 32 (over z, x_lo, core), bl: 8 (over y, x_hi).
Axes of the slice: x: 4 (x_hi: 2, x_lo: 2; x = x_hi * 2 + x_lo), y: 4, z: 8, core: 2. Of those that a mesh axis runs over, the one named last changes fastest.
Arguments:
- visibilities: bfloat16 [2, 16640, 8192], P(None, 'bl', 'ma'), may hold values from -6 to 6
- beam_blocks: bfloat16 [32, 2, 16640, 1000], P('ma', None, 'bl'), may hold values from -0.0625 to 0.0625
- feed_pairs: int32 [16640, 2], P('bl'), may hold values from 0 to 1023
- feed_gains: float32 [2, 1024], replicated, may hold values from -1.5 to 1.5
- m_order: int32 [32], replicated, may hold values from 0 to 31, each once
Outputs:
- sky_modes: float32 [2, 32, 1000], P(None, 'ma', 'bl')
All inputs are finite; a program needn't handle non-finite values.
Results may differ from a plain program's by a relative error of at most 0.0049.
Values may be sent and summed in bfloat16 or wider, within the bound.
No kernel may reach another device: no remote copies, remote signals or barrier semaphores. Data moves between devices by JAX's collectives and lax.ppermute only.
A program may use at most 64 MiB of HBM per device.

v0:
```python
import jax
import jax.numpy as jnp
from jax import lax
from jax.sharding import PartitionSpec as P

NT = 8192


def dft_weights(time_index, m_values):
    wrapped = jnp.mod(time_index[:, None] * m_values[None, :], NT).astype(jnp.float32)
    phases = wrapped * (2.0 * jnp.pi / NT)
    scale = 1.0 / jnp.sqrt(jnp.float32(NT))
    cos_part = (jnp.cos(phases) * scale).astype(jnp.bfloat16)
    sin_part = (jnp.sin(phases) * scale).astype(jnp.bfloat16)
    upper = jnp.concatenate([cos_part, -sin_part], axis=1)
    lower = jnp.concatenate([sin_part, cos_part], axis=1)
    return jnp.concatenate([upper, lower], axis=0)


def transform(visible, weights, count):
    stacked_in = jnp.concatenate([visible[0], visible[1]], axis=1)
    flat = jnp.dot(stacked_in, weights, preferred_element_type=jnp.float32)
    return jnp.stack([flat[:, :count], flat[:, count:]])


def per_device(visibilities, beam_blocks, feed_pairs, feed_gains, m_order):
    count = m_order.shape[0]
    m_values = m_order - count // 2
    turned = lax.all_to_all(visibilities, "ma", split_axis=1, concat_axis=2, tiled=True)
    time_index = jnp.arange(NT, dtype=jnp.int32)
    weights = dft_weights(time_index, m_values)
    spectra_all = transform(turned, weights, count).astype(jnp.bfloat16)
    owned = lax.all_to_all(spectra_all, "ma", split_axis=2, concat_axis=1, tiled=True)
    local_rows = feed_pairs.shape[0]
    feed_count = feed_gains.shape[1]
    both_feeds = jnp.concatenate([feed_pairs[:, 0], feed_pairs[:, 1]], axis=0)
    feed_iota = jnp.arange(feed_count, dtype=jnp.int32)
    one_hot = (both_feeds[:, None] == feed_iota[None, :]).astype(jnp.float32)
    picked = jnp.dot(
        one_hot,
        jnp.transpose(feed_gains),
        precision=lax.Precision.HIGHEST,
        preferred_element_type=jnp.float32,
    )
    a_re = picked[:local_rows, 0]
    a_im = picked[:local_rows, 1]
    b_re = picked[local_rows:, 0]
    b_im = picked[local_rows:, 1]
    factor_re = (a_re * b_re + a_im * b_im)[:, None]
    factor_im = (a_im * b_re - a_re * b_im)[:, None]
    spec_re = owned[0].astype(jnp.float32)
    spec_im = owned[1].astype(jnp.float32)
    weighted_re = (spec_re * factor_re - spec_im * factor_im).astype(jnp.bfloat16)
    weighted_im = (spec_re * factor_im + spec_im * factor_re).astype(jnp.bfloat16)
    row_real = jnp.concatenate([weighted_re, weighted_im], axis=0)
    row_imag = jnp.concatenate([weighted_im, -weighted_re], axis=0)
    vectors = jnp.transpose(jnp.stack([row_real, row_imag]), (2, 0, 1))
    local_modes = beam_blocks.shape[0]
    block_rows = beam_blocks.shape[2]
    width = beam_blocks.shape[3]
    flat_blocks = beam_blocks.reshape(local_modes, 2 * block_rows, width)
    partial_value = jnp.einsum(
        "mkc,mcl->kml", vectors, flat_blocks, preferred_element_type=jnp.float32
    )
    totals = lax.psum(partial_value, "bl")
    share_width = width // lax.axis_size("bl")
    result = lax.dynamic_slice_in_dim(totals, lax.axis_index("bl") * share_width, share_width, 2)
    return result


def solution(mesh):
    return jax.shard_map(
        per_device,
        mesh=mesh,
        in_specs=(P(None, "bl", "ma"), P("ma", None, "bl", None), P("bl", None), P(), P()),
        out_specs=P(None, "ma", "bl"),
        check_vma=False,
    )
```

profile of v0, /device:TPU:32, one launch (start us, length us, event | category | flops | bytes accessed | tf_op | source)
XLA Modules:
  0.0 125.1 jit_solution(16303524143769065953)
XLA Ops:
  0.0 14.5 %copy.16 = bf16[2,2080,256]{2,0,1:T(2,128)(2,1)} copy(bf16[2,2080,256]{2,1,0:T(8,128)(2,1)} %param.5) | data formatting | bytes 4259840 | tf_op args[0]
  14.5 9.8 %all-to-all-start = ((bf16[2,2080,256]{2,0,1:T(2,128)(2,1)}), bf16[2,2080,256]{2,0,1:T(2,128)(2,1)S(1)}, u32[]{:S(2)}, u32[]{:S(2)}) async-start(bf16[2,2080,256]{2,0,1:T(2,128)(2,1)} %copy.16), calls=%async_computation | async-start | bytes 4259840 | tf_op jit(solution)/shard_map/all_to_all | solution.py:29
  24.4 4.2 %fusion.24 = bf16[8192,32]{0,1:T(8,128)(2,1)S(1)} fusion(s32[32]{0:T(128)S(1)} %broadcast_add_fusion), kind=kLoop, calls=%fused_computation.29 | loop fusion | flops 4980736 | bytes 524416 | tf_op jit(solution)/shard_map/neg | solution.py:15
  28.7 5.2 %multiply_convert_fusion = (bf16[8192,32]{0,1:T(8,128)(2,1)S(1)}, bf16[8192,32]{0,1:T(8,128)(2,1)}) fusion(s32[32]{0:T(128)S(1)} %broadcast_add_fusion), kind=kLoop, calls=%fused_computation.24 | loop fusion | flops 4718592 | bytes 1048704 | tf_op jit(solution)/shard_map/convert_element_type | solution.py:14
  33.9 41.6 %all-to-all-done = bf16[2,2080,256]{2,0,1:T(2,128)(2,1)S(1)} async-done(((bf16[2,2080,256]{2,0,1:T(2,128)(2,1)}), bf16[2,2080,256]{2,0,1:T(2,128)(2,1)S(1)}, u32[]{:S(2)}, u32[]{:S(2)}) %all-to-all-start) | async-done | bytes 2129952 | tf_op jit(solution)/shard_map/all_to_all | solution.py:29
  75.5 3.0 %fusion.31 = (bf16[1,65,32,256]{3,0,1,2:T(2,128)(2,1)S(1)}, bf16[1,65,32,256]{3,0,1,2:T(2,128)(2,1)S(1)}) fusion(bf16[2,65,32,256]{3,0,1,2:T(2,128)(2,1)S(1)} %bitcast.38), kind=kLoop, calls=%fused_computation.53 | loop fusion | bytes 4259840 | tf_op jit(solution)/shard_map/slice | solution.py:21
  78.5 0.6 copy_bitcast_fusion
  79.1 0.1 pad.16
  79.2 0.7 copy.22
  80.0 0.1 pad.17
  80.1 0.7 copy.23
  80.8 0.2 copy-done.1
  81.0 0.9 fusion.13
  81.9 0.6 copy.19
  82.6 4.4 %all-to-all-start.1 = ((bf16[2,65,32]{1,0,2:T(2,128)(2,1)}), bf16[2,65,32]{1,0,2:T(2,128)(2,1)S(1)}, u32[]{:S(2)}, u32[]{:S(2)}) async-start(bf16[2,65,32]{1,0,2:T(2,128)(2,1)} %copy.19), calls=%async_computation.1 | async-start | bytes 32768 | tf_op jit(solution)/shard_map/all_to_all | solution.py:33
  87.0 7.6 %fusion = f32[4160,2]{0,1:T(2,128)S(1)} fusion(f32[2,1024]{1,0:T(2,128)S(1)} %copy-done, s32[4160]{0:T(1024)S(1)} %pad_add_fusion), kind=kOutput, calls=%fused_computation.1 | convolution fusion | flops 106496000 | bytes 58112 | tf_op jit(solution)/shard_map/dot_general | solution.py:39
  94.6 0.1 fusion.28
  94.7 0.1 reshape.63
  94.8 0.1 reshape.64
  94.9 0.1 add_convert_fusion
  95.1 0.1 maximum_bitcast_fusion
  95.2 4.6 %convolution_bitcast_fusion = f32[2,1,1000]{2,0,1:T(2,128)S(1)} fusion(bf16[4160,1000]{1,0:T(8,128)(2,1)} %bitcast.37, bf16[2,4160,1]{1,2,0:T(2,128)(2,1)S(1)} %pad_maximum_fusion), kind=kOutput, calls=%fused_computation.18 | convolution fusion | flops 16640000 | bytes 8344640 | tf_op jit(solution)/shard_map/mkc,mcl->kml/dot_general | solution.py:62
  99.9 24.6 %psum.7 = f32[2,1,1000]{2,0,1:T(2,128)S(1)} all-reduce(f32[2,1,1000]{2,0,1:T(2,128)S(1)} %convolution_bitcast_fusion), channel_id=1, replica_groups=mesh['ma'=32,'bl'=8] {'bl'}, use_global_device_ids=true, to_apply=%region_0.1 | all-reduce | flops 2000 | bytes 16000 | tf_op jit(solution)/shard_map/psum | solution.py:65
  124.4 0.6 constant_dynamic-slice_fusion
  (15 shorter events, 0.2 us)
Async XLA Ops:
  0.0 87.0 %copy-start = (f32[2,1024]{1,0:T(2,128)S(1)}, f32[2,1024]{1,0:T(2,128)}, u32[]{:S(2)}) copy-start(f32[2,1024]{1,0:T(2,128)} %param.8) | copy-start | bytes 24580
  14.5 9.8 %copy-start.2 = (s32[2080,2]{0,1:T(2,128)S(1)}, s32[2080,2]{0,1:T(2,128)}, u32[]{:S(2)}) copy-start(s32[2080,2]{0,1:T(2,128)} %param.7) | copy-start | bytes 49924
  14.5 9.9 %copy-start.3 = (s32[32]{0:T(128)S(1)}, s32[32]{0:T(128)}, u32[]{:S(2)}) copy-start(s32[32]{0:T(128)} %param.9) | copy-start | bytes 388
  14.5 61.0 %all-to-all-start = ((bf16[2,2080,256]{2,0,1:T(2,128)(2,1)}), bf16[2,2080,256]{2,0,1:T(2,128)(2,1)S(1)}, u32[]{:S(2)}, u32[]{:S(2)}) async-start(bf16[2,2080,256]{2,0,1:T(2,128)(2,1)} %copy.16), calls=%async_computation | async-start | bytes 4259840 | tf_op jit(solution)/shard_map/all_to_all | solution.py:29
  80.0 1.0 copy-start.1
  82.6 12.0 %all-to-all-start.1 = ((bf16[2,65,32]{1,0,2:T(2,128)(2,1)}), bf16[2,65,32]{1,0,2:T(2,128)(2,1)S(1)}, u32[]{:S(2)}, u32[]{:S(2)}) async-start(bf16[2,65,32]{1,0,2:T(2,128)(2,1)} %copy.19), calls=%async_computation.1 | async-start | bytes 32768 | tf_op jit(solution)/shard_map/all_to_all | solution.py:33
where the time goes:
time: 125 us
  waiting for transfers between devices  41.6 us (33%)
  blocking collectives  24.6 us (20%)
  local copies, waits for them, and re-layouts  21.5 us (17%)
  starting transfers between devices  14.2 us (11%)
  matrix products  13.1 us (10%)
  other arithmetic  9.93 us (8%)
    all_to_all x1, waiting for transfers between devices, per_device(): lax.all_to_all(visibilities, 'ma', split_axis=1, concat_axis=2, tiled=True)  41.6 us
    psum x1, blocking collectives, per_device(): totals = lax.psum(partial_value, 'bl')  24.6 us
    unnamed x14, local copies, waits for them, and re-layouts  16.9 us
    all_to_all x1, starting transfers between devices, per_device(): lax.all_to_all(visibilities, 'ma', split_axis=1, concat_axis=2, tiled=True)  9.79 us
    dot_general x1, matrix products, per_device(): jnp.dot(one_hot, jnp.transpose(feed_gains), precision=lax.Precision.HIGHE...  7.6 us
    convert_element_type x1, other arithmetic, dft_weights(): sin_part = (jnp.sin(phases) * scale).astype(jnp.bfloat16)  5.22 us
    dot_general x1, matrix products, per_device(): jnp.einsum('mkc,mcl->kml', vectors, flat_blocks, preferred_element_type=j...  4.63 us
    all_to_all x1, starting transfers between devices, per_device(): lax.all_to_all(spectra_all, 'ma', split_axis=2, concat_axis=1, tiled=True)  4.41 us
  transfers between devices with their start and end apart: 2, of which 1 were waited for; matrix products, arithmetic and copies ran while one was open for 14% of the time, Pallas kernels for 0%

commit v1 on v0

--- a/solution.py
+++ b/solution.py
@@ -26,7 +26,10 @@
 def per_device(visibilities, beam_blocks, feed_pairs, feed_gains, m_order):
     count = m_order.shape[0]
     m_values = m_order - count // 2
-    turned = lax.all_to_all(visibilities, "ma", split_axis=1, concat_axis=2, tiled=True)
+    turned = jnp.concatenate(
+        lax.all_to_all(jnp.stack(jnp.split(visibilities, lax.axis_size("ma"), axis=1)), "ma", 0, 0),
+        axis=2,
+    )
     time_index = jnp.arange(NT, dtype=jnp.int32)
     weights = dft_weights(time_index, m_values)
     spectra_all = transform(turned, weights, count).astype(jnp.bfloat16)

time: 125 us -> 136 us (1.088)
  local copies, waits for them, and re-layouts: 21.5 us -> 32.3 us
    unnamed x14 -> x44, local copies, waits for them, and re-layouts: 16.9 us -> 23.4 us
    split x0 -> x2, local copies, waits for them, and re-layouts: none -> 3.69 us  [per_device(): jnp.split(visibilities, lax.axis_size('ma'), axis=1)]
  transfers between devices with their start and end apart: 2 -> 2, of which waited for: 1 -> 1; matrix products, arithmetic and copies ran while one was open for 14% -> 13% of each run, Pallas kernels for 0% -> 0%
where the time goes in v1:
time: 136 us
  waiting for transfers between devices  41.6 us (31%)
  local copies, waits for them, and re-layouts  32.3 us (24%)
  blocking collectives  24.6 us (18%)
  starting transfers between devices  14.2 us (10%)
  matrix products  13.1 us (10%)
  other arithmetic  9.93 us (7%)
    all_to_all x1, waiting for transfers between devices, per_device(): lax.all_to_all(jnp.stack(jnp.split(visibilities, lax.axis_size('ma'), axi...  41.6 us
    psum x1, blocking collectives, per_device(): totals = lax.psum(partial_value, 'bl')  24.6 us
    unnamed x44, local copies, waits for them, and re-layouts  23.4 us
    all_to_all x1, starting transfers between devices, per_device(): lax.all_to_all(jnp.stack(jnp.split(visibilities, lax.axis_size('ma'), axi...  9.79 us
    dot_general x1, matrix products, per_device(): jnp.dot(one_hot, jnp.transpose(feed_gains), precision=lax.Precision.HIGHE...  7.6 us
    convert_element_type x1, other arithmetic, dft_weights(): sin_part = (jnp.sin(phases) * scale).astype(jnp.bfloat16)  5.22 us
    dot_general x1, matrix products, per_device(): jnp.einsum('mkc,mcl->kml', vectors, flat_blocks, preferred_element_type=j...  4.63 us
    all_to_all x1, starting transfers between devices, per_device(): lax.all_to_all(spectra_all, 'ma', split_axis=2, concat_axis=1, tiled=True)  4.41 us
  transfers between devices with their start and end apart: 2, of which 1 were waited for; matrix products, arithmetic and copies ran while one was open for 13% of the time, Pallas kernels for 0%

profile of v1, /device:TPU:32, one launch (start us, length us, event | category | flops | bytes accessed | tf_op | source)
XLA Modules:
  0.0 136.0 jit_solution(15307813368048357756)
XLA Ops:
  0.0 1.6 %fusion.33 = (bf16[2,65,256]{2,1,0:T(8,128)(2,1)S(1)}, bf16[2,65,256]{2,1,0:T(8,128)(2,1)S(1)}, bf16[2,65,256]{2,1,0:T(8,128)(2,1)S(1)}, bf16[2,65,256]{2,1,0:T(...) fusion(bf16[2,2080,256]{2,1,0:T(8,128)(2,1)} %param.5), kind=kLoop, calls=%fused_computation.119 | loop fusion | bytes 1730560 | tf_op jit(solution)/shard_map/split | solution.py:30
  1.6 2.0 %fusion.32 = (bf16[2,65,256]{2,1,0:T(8,128)(2,1)S(1)}, bf16[2,65,256]{2,1,0:T(8,128)(2,1)S(1)}, bf16[2,65,256]{2,1,0:T(8,128)(2,1)S(1)}, bf16[2,65,256]{2,1,0:T(...) fusion(bf16[2,2080,256]{2,1,0:T(8,128)(2,1)} %param.5), kind=kLoop, calls=%fused_computation.118 | loop fusion | bytes 2529280 | tf_op jit(solution)/shard_map/split | solution.py:30
  4.4 0.7 constant_dynamic-update-slice_fusion.30
  5.0 0.7 constant_dynamic-update-slice_fusion.29
  5.7 0.7 constant_dynamic-update-slice_fusion.28
  8.4 0.7 constant_dynamic-update-slice_fusion.24
  9.1 0.7 constant_dynamic-update-slice_fusion.23
  16.5 0.7 constant_dynamic-update-slice_fusion.12
  17.9 0.7 constant_dynamic-update-slice_fusion.10
  22.6 0.7 constant_dynamic-update-slice_fusion.3
  23.3 0.7 constant_dynamic-update-slice_fusion.2
  24.7 0.7 constant_dynamic-update-slice_fusion
  25.4 9.8 %all-to-all-start = ((bf16[32,2,65,256]{3,1,2,0:T(2,128)(2,1)}), bf16[32,2,65,256]{3,1,2,0:T(2,128)(2,1)S(1)}, u32[]{:S(2)}, u32[]{:S(2)}) async-start(bf16[32,2,65,256]{3,1,2,0:T(2,128)(2,1)} %constant_dynamic-update-slice_fusion), calls=%async_computation | async-start | bytes 4259840 | tf_op jit(solution)/shard_map/all_to_all | solution.py:30
  35.3 4.2 %fusion.24 = bf16[8192,32]{0,1:T(8,128)(2,1)S(1)} fusion(s32[32]{0:T(128)S(1)} %broadcast_add_fusion), kind=kLoop, calls=%fused_computation.29 | loop fusion | flops 4980736 | bytes 524416 | tf_op jit(solution)/shard_map/neg | solution.py:15
  39.6 5.2 %multiply_convert_fusion = (bf16[8192,32]{0,1:T(8,128)(2,1)S(1)}, bf16[8192,32]{0,1:T(8,128)(2,1)}) fusion(s32[32]{0:T(128)S(1)} %broadcast_add_fusion), kind=kLoop, calls=%fused_computation.24 | loop fusion | flops 4718592 | bytes 1048704 | tf_op jit(solution)/shard_map/convert_element_type | solution.py:14
  44.8 41.6 %all-to-all-done = bf16[32,2,65,256]{3,1,2,0:T(2,128)(2,1)S(1)} async-done(((bf16[32,2,65,256]{3,1,2,0:T(2,128)(2,1)}), bf16[32,2,65,256]{3,1,2,0:T(2,128)(2,1)S(1)}, u32[]{:S(2)}, u32[]{:S(2)}) %all-to-all-start) | async-done | bytes 2129952 | tf_op jit(solution)/shard_map/all_to_all | solution.py:30
  86.4 3.0 %fusion.31 = (bf16[1,65,32,256]{3,0,1,2:T(2,128)(2,1)S(1)}, bf16[1,65,32,256]{3,0,1,2:T(2,128)(2,1)S(1)}) fusion(bf16[2,65,32,256]{3,0,1,2:T(2,128)(2,1)S(1)} %bitcast.164), kind=kLoop, calls=%fused_computation.117 | loop fusion | bytes 4259840 | tf_op jit(solution)/shard_map/slice | solution.py:21
  90.1 0.7 copy.115
  91.0 0.7 copy.116
  91.9 0.9 fusion.13
  93.4 4.4 %all-to-all-start.1 = ((bf16[2,65,32]{1,0,2:T(2,128)(2,1)}), bf16[2,65,32]{1,0,2:T(2,128)(2,1)S(1)}, u32[]{:S(2)}, u32[]{:S(2)}) async-start(bf16[2,65,32]{1,0,2:T(2,128)(2,1)} %copy.80), calls=%async_computation.1 | async-start | bytes 32768 | tf_op jit(solution)/shard_map/all_to_all | solution.py:36
  97.9 7.6 %fusion = f32[4160,2]{0,1:T(2,128)S(1)} fusion(f32[2,1024]{1,0:T(2,128)S(1)} %copy-done, s32[4160]{0:T(1024)S(1)} %pad_add_fusion), kind=kOutput, calls=%fused_computation.1 | convolution fusion | flops 106496000 | bytes 58112 | tf_op jit(solution)/shard_map/dot_general | solution.py:42
  106.1 4.6 %convolution_bitcast_fusion = f32[2,1,1000]{2,0,1:T(2,128)S(1)} fusion(bf16[4160,1000]{1,0:T(8,128)(2,1)} %bitcast.163, bf16[2,4160,1]{1,2,0:T(2,128)(2,1)S(1)} %pad_maximum_fusion), kind=kOutput, calls=%fused_computation.18 | convolution fusion | flops 16640000 | bytes 8344640 | tf_op jit(solution)/shard_map/mkc,mcl->kml/dot_general | solution.py:65
  110.7 24.6 %psum.7 = f32[2,1,1000]{2,0,1:T(2,128)S(1)} all-reduce(f32[2,1,1000]{2,0,1:T(2,128)S(1)} %convolution_bitcast_fusion), channel_id=1, replica_groups=mesh['ma'=32,'bl'=8] {'bl'}, use_global_device_ids=true, to_apply=%region_0.1 | all-reduce | flops 2000 | bytes 16000 | tf_op jit(solution)/shard_map/psum | solution.py:68
  (48 shorter events, 17.8 us)
Async XLA Ops:
  0.0 97.9 %copy-start = (f32[2,1024]{1,0:T(2,128)S(1)}, f32[2,1024]{1,0:T(2,128)}, u32[]{:S(2)}) copy-start(f32[2,1024]{1,0:T(2,128)} %param.8) | copy-start | bytes 24580
  25.4 9.8 %copy-start.2 = (s32[2080,2]{0,1:T(2,128)S(1)}, s32[2080,2]{0,1:T(2,128)}, u32[]{:S(2)}) copy-start(s32[2080,2]{0,1:T(2,128)} %param.7) | copy-start | bytes 49924
  25.4 9.9 %copy-start.3 = (s32[32]{0:T(128)S(1)}, s32[32]{0:T(128)}, u32[]{:S(2)}) copy-start(s32[32]{0:T(128)} %param.9) | copy-start | bytes 388
  25.4 61.0 %all-to-all-start = ((bf16[32,2,65,256]{3,1,2,0:T(2,128)(2,1)}), bf16[32,2,65,256]{3,1,2,0:T(2,128)(2,1)S(1)}, u32[]{:S(2)}, u32[]{:S(2)}) async-start(bf16[32,2,65,256]{3,1,2,0:T(2,128)(2,1)} %constant_dynamic-update-slice_fusion), calls=%async_computation | async-start | bytes 4259840 | tf_op jit(solution)/shard_map/all_to_all | solution.py:30
  90.8 1.0 copy-start.1
  93.4 12.0 %all-to-all-start.1 = ((bf16[2,65,32]{1,0,2:T(2,128)(2,1)}), bf16[2,65,32]{1,0,2:T(2,128)(2,1)S(1)}, u32[]{:S(2)}, u32[]{:S(2)}) async-start(bf16[2,65,32]{1,0,2:T(2,128)(2,1)} %copy.80), calls=%async_computation.1 | async-start | bytes 32768 | tf_op jit(solution)/shard_map/all_to_all | solution.py:36

commit v2 on v0

--- a/solution.py
+++ b/solution.py
@@ -62,7 +62,7 @@
     partial_value = jnp.einsum(
         "mkc,mcl->kml", vectors, flat_blocks, preferred_element_type=jnp.float32
     )
-    totals = lax.psum(partial_value, "bl")
+    totals = jnp.sum(lax.all_gather(partial_value, "bl"), axis=0)
     share_width = width // lax.axis_size("bl")
     result = lax.dynamic_slice_in_dim(totals, lax.axis_index("bl") * share_width, share_width, 2)
     return result

time: 125 us -> 136 us (1.088)
  blocking collectives: 24.6 us -> 34.6 us
    all_gather x0 -> x1, blocking collectives: none -> 34.6 us  [per_device(): totals = jnp.sum(lax.all_gather(partial_value, 'bl'), axis=0)]
    psum x1 -> x0, blocking collectives: 24.6 us -> none  [per_device(): totals = lax.psum(partial_value, 'bl')]
  transfers between devices with their start and end apart: 2 -> 2, of which waited for: 1 -> 1; matrix products, arithmetic and copies ran while one was open for 14% -> 13% of each run, Pallas kernels for 0% -> 0%
where the time goes in v2:
time: 136 us; the launch traced here: 135 us
  waiting for transfers between devices  41.6 us (31%)
  blocking collectives  34.6 us (25%)
  local copies, waits for them, and re-layouts  21.5 us (16%)
  starting transfers between devices  14.2 us (10%)
  matrix products  13.1 us (10%)
  other arithmetic  10.1 us (7%)
    all_to_all x1, waiting for transfers between devices, per_device(): lax.all_to_all(visibilities, 'ma', split_axis=1, concat_axis=2, tiled=True)  41.6 us
    all_gather x1, blocking collectives, per_device(): totals = jnp.sum(lax.all_gather(partial_value, 'bl'), axis=0)  34.6 us
    unnamed x14, local copies, waits for them, and re-layouts  16.9 us
    all_to_all x1, starting transfers between devices, per_device(): lax.all_to_all(visibilities, 'ma', split_axis=1, concat_axis=2, tiled=True)  9.79 us
    dot_general x1, matrix products, per_device(): jnp.dot(one_hot, jnp.transpose(feed_gains), precision=lax.Precision.HIGHE...  7.6 us
    convert_element_type x1, other arithmetic, dft_weights(): sin_part = (jnp.sin(phases) * scale).astype(jnp.bfloat16)  5.23 us
    dot_general x1, matrix products, per_device(): jnp.einsum('mkc,mcl->kml', vectors, flat_blocks, preferred_element_type=j...  4.63 us
    all_to_all x1, starting transfers between devices, per_device(): lax.all_to_all(spectra_all, 'ma', split_axis=2, concat_axis=1, tiled=True)  4.41 us
  transfers between devices with their start and end apart: 2, of which 1 were waited for; matrix products, arithmetic and copies ran while one was open for 13% of the time, Pallas kernels for 0%

profile of v2, /device:TPU:32, one launch (start us, length us, event | category | flops | bytes accessed | tf_op | source)
XLA Modules:
  0.0 135.3 jit_solution(5022039989409047522)
XLA Ops:
  0.0 14.5 %copy.14 = bf16[2,2080,256]{2,0,1:T(2,128)(2,1)} copy(bf16[2,2080,256]{2,1,0:T(8,128)(2,1)} %param.5) | data formatting | bytes 4259840 | tf_op args[0]
  14.5 9.8 %all-to-all-start = ((bf16[2,2080,256]{2,0,1:T(2,128)(2,1)}), bf16[2,2080,256]{2,0,1:T(2,128)(2,1)S(1)}, u32[]{:S(2)}, u32[]{:S(2)}) async-start(bf16[2,2080,256]{2,0,1:T(2,128)(2,1)} %copy.14), calls=%async_computation | async-start | bytes 4259840 | tf_op jit(solution)/shard_map/all_to_all | solution.py:29
  24.4 4.2 %fusion.24 = bf16[8192,32]{0,1:T(8,128)(2,1)S(1)} fusion(s32[32]{0:T(128)S(1)} %broadcast_add_fusion), kind=kLoop, calls=%fused_computation.29 | loop fusion | flops 4980736 | bytes 524416 | tf_op jit(solution)/shard_map/neg | solution.py:15
  28.7 5.2 %multiply_convert_fusion = (bf16[8192,32]{0,1:T(8,128)(2,1)S(1)}, bf16[8192,32]{0,1:T(8,128)(2,1)}) fusion(s32[32]{0:T(128)S(1)} %broadcast_add_fusion), kind=kLoop, calls=%fused_computation.24 | loop fusion | flops 4718592 | bytes 1048704 | tf_op jit(solution)/shard_map/convert_element_type | solution.py:14
  33.9 41.6 %all-to-all-done = bf16[2,2080,256]{2,0,1:T(2,128)(2,1)S(1)} async-done(((bf16[2,2080,256]{2,0,1:T(2,128)(2,1)}), bf16[2,2080,256]{2,0,1:T(2,128)(2,1)S(1)}, u32[]{:S(2)}, u32[]{:S(2)}) %all-to-all-start) | async-done | bytes 2129952 | tf_op jit(solution)/shard_map/all_to_all | solution.py:29
  75.5 3.0 %fusion.31 = (bf16[1,65,32,256]{3,0,1,2:T(2,128)(2,1)S(1)}, bf16[1,65,32,256]{3,0,1,2:T(2,128)(2,1)S(1)}) fusion(bf16[2,65,32,256]{3,0,1,2:T(2,128)(2,1)S(1)} %bitcast.38), kind=kLoop, calls=%fused_computation.53 | loop fusion | bytes 4259840 | tf_op jit(solution)/shard_map/slice | solution.py:21
  78.5 0.6 copy_bitcast_fusion
  79.1 0.1 pad.16
  79.2 0.7 copy.21
  80.0 0.1 pad.17
  80.1 0.7 copy.22
  80.8 0.2 copy-done.1
  81.0 0.9 fusion.13
  82.0 0.6 copy.17
  82.6 4.4 %all-to-all-start.1 = ((bf16[2,65,32]{1,0,2:T(2,128)(2,1)}), bf16[2,65,32]{1,0,2:T(2,128)(2,1)S(1)}, u32[]{:S(2)}, u32[]{:S(2)}) async-start(bf16[2,65,32]{1,0,2:T(2,128)(2,1)} %copy.17), calls=%async_computation.1 | async-start | bytes 32768 | tf_op jit(solution)/shard_map/all_to_all | solution.py:33
  87.0 7.6 %fusion = f32[4160,2]{0,1:T(2,128)S(1)} fusion(f32[2,1024]{1,0:T(2,128)S(1)} %copy-done, s32[4160]{0:T(1024)S(1)} %pad_add_fusion), kind=kOutput, calls=%fused_computation.1 | convolution fusion | flops 106496000 | bytes 58112 | tf_op jit(solution)/shard_map/dot_general | solution.py:39
  94.6 0.1 fusion.28
  94.7 0.1 reshape.65
  94.8 0.1 reshape.66
  94.9 0.1 add_convert_fusion
  95.2 4.6 %convolution_bitcast_fusion = f32[2,1,1000]{2,0,1:T(2,128)S(1)} fusion(bf16[4160,1000]{1,0:T(8,128)(2,1)} %bitcast.37, bf16[2,4160,1]{1,2,0:T(2,128)(2,1)S(1)} %pad_maximum_fusion), kind=kOutput, calls=%fused_computation.18 | convolution fusion | flops 16640000 | bytes 8344640 | tf_op jit(solution)/shard_map/mkc,mcl->kml/dot_general | solution.py:62
  99.9 34.6 %all-gather = f32[16,1,1000]{2,1,0:T(1,128)S(1)} all-gather(f32[2,1,1000]{2,1,0:T(1,128)S(1)} %copy.18), channel_id=2, replica_groups=mesh['ma'=32,'bl'=8] {'bl'}, dimensions={0}, use_global_device_ids=true | all-gather | bytes 72000 | tf_op jit(solution)/shard_map/all_gather | solution.py:65
  134.5 0.2 reduce.6
  134.7 0.6 constant_dynamic-slice_fusion
  (19 shorter events, 0.4 us)
Async XLA Ops:
  0.0 87.0 %copy-start = (f32[2,1024]{1,0:T(2,128)S(1)}, f32[2,1024]{1,0:T(2,128)}, u32[]{:S(2)}) copy-start(f32[2,1024]{1,0:T(2,128)} %param.8) | copy-start | bytes 24580
  14.5 9.8 %copy-start.2 = (s32[2080,2]{0,1:T(2,128)S(1)}, s32[2080,2]{0,1:T(2,128)}, u32[]{:S(2)}) copy-start(s32[2080,2]{0,1:T(2,128)} %param.7) | copy-start | bytes 49924
  14.5 9.9 %copy-start.3 = (s32[32]{0:T(128)S(1)}, s32[32]{0:T(128)}, u32[]{:S(2)}) copy-start(s32[32]{0:T(128)} %param.9) | copy-start | bytes 388
  14.5 61.0 %all-to-all-start = ((bf16[2,2080,256]{2,0,1:T(2,128)(2,1)}), bf16[2,2080,256]{2,0,1:T(2,128)(2,1)S(1)}, u32[]{:S(2)}, u32[]{:S(2)}) async-start(bf16[2,2080,256]{2,0,1:T(2,128)(2,1)} %copy.14), calls=%async_computation | async-start | bytes 4259840 | tf_op jit(solution)/shard_map/all_to_all | solution.py:29
  80.0 1.0 copy-start.1
  82.6 12.0 %all-to-all-start.1 = ((bf16[2,65,32]{1,0,2:T(2,128)(2,1)}), bf16[2,65,32]{1,0,2:T(2,128)(2,1)S(1)}, u32[]{:S(2)}, u32[]{:S(2)}) async-start(bf16[2,65,32]{1,0,2:T(2,128)(2,1)} %copy.17), calls=%async_computation.1 | async-start | bytes 32768 | tf_op jit(solution)/shard_map/all_to_all | solution.py:33
